TPU v7x, 128 devices: a whole 4x4x4 slice. The times are simulated.
128 devices in a mesh: group: 8 (over x, core), sub: 16 (over z, y).
Axes of the slice: x: 4, y: 4, z: 4, core: 2. Of those that a mesh axis runs over, the one named last changes fastest.
Arguments:
- schur: bfloat16 [8, 16, 1024, 1024], P('group', 'sub'), as said below
- local_inverse: bfloat16 [8, 16, 1024, 1024], P('group', 'sub'), as said below
- rhs_parts: bfloat16 [8, 16, 1024, 128], P('group', 'sub'), may hold values from -6 to 6
- basis: bfloat16 [8, 16, 32, 1024], P('group', 'sub'), may hold values from -0.1875 to 0.1875
- coarse_map: int32 [8, 16, 32], P('group', 'sub'), may hold values from 0 to 1023
- coarse_inverse: bfloat16 [8, 1024, 1024], P('group', 'sub'), as said below
- shared_rows: int32 [8, 16, 2, 4, 256], P('group', 'sub'), may hold values from 0 to 1023, as said below
- shared_counts: int32 [8, 16, 4], P('group', 'sub'), may hold values from 0 to 256, as said below
Outputs:
- solution: float32 [8, 16, 1024, 128], P('group', 'sub')
- residual: float32 [8, 16, 1024, 128], P('group', 'sub')
Inputs may be any that keep to these rules, and one draw needn't show every extreme that they name: `schur`: each subdomain matrix is symmetric positive definite. `local_inverse`: each subdomain matrix is symmetric positive definite. `coarse_inverse`: each group's matrix is symmetric positive definite. `shared_rows`: own rows of direction d lie in rows d * 256 to (d + 1) * 256 - 1 and are distinct within a list; the own rows of direction 0 of (g, s) are the partner rows of direction 1 of (g, s + 1) and the reverse, likewise directions 2 and 3 between (g, s) and (g + 1, s); entries past the count are rows of the same block. `shared_counts`: the count of direction 0 of (g, s) equals the count of direction 1 of (g, s + 1), that of direction 2 of (g, s) the count of direction 3 of (g + 1, s); counts are 0 where no neighbour exists; some count equals 256.
All inputs are finite; a program needn't handle non-finite values.
Results may differ from a plain program's by a relative error of at most 0.014.
Values may be sent and summed in bfloat16 or wider, within the bound.
A program may use at most 64 MiB of HBM per device.

v0:
```python
import jax
import jax.numpy as jnp
from jax import lax
from jax.sharding import PartitionSpec as P

ITERS = 3


def extended(block, sides, width):
    for axis, dim in sides:
        count = lax.axis_size(axis)
        forward = [(i, i + 1) for i in range(count - 1)]
        backward = [(target, source) for source, target in forward]
        low = lax.ppermute(
            lax.slice_in_dim(block, block.shape[dim] - width, None, axis=dim), axis, forward
        )
        high = lax.ppermute(lax.slice_in_dim(block, 0, width, axis=dim), axis, backward)
        block = jnp.concatenate([low, block, high], axis=dim)
    return block


def pick_rows(tables, indices):
    return jax.vmap(jax.vmap(lambda source_block, rows_at: source_block[rows_at]))(tables, indices)


def add_rows(bases, indices, additions):

    def add_single(base_block, rows_at, extra):
        return base_block.at[rows_at.reshape(-1)].add(extra.reshape(-1, base_block.shape[-1]))

    return jax.vmap(jax.vmap(add_single))(bases, indices, additions)


def count_rows(indices, live_mask, rows_local):

    def count_single(rows_at, mask_rows):
        return (
            jnp.ones((rows_local,), jnp.float32).at[rows_at.reshape(-1)].add(mask_rows.reshape(-1))
        )

    return jax.vmap(jax.vmap(count_single))(indices, live_mask)


def assemble(blocks, own_rows, partner_rows, live_mask):
    padded = extended(blocks, (("group", 0), ("sub", 1)), 1)
    received = jnp.stack(
        [
            pick_rows(padded[1:2, 2:], partner_rows[:, :, 0]),
            pick_rows(padded[1:2, :-2], partner_rows[:, :, 1]),
            pick_rows(padded[2:3, 1:-1], partner_rows[:, :, 2]),
            pick_rows(padded[0:1, 1:-1], partner_rows[:, :, 3]),
        ],
        axis=2,
    )
    values = received * live_mask[..., None]
    return add_rows(blocks, own_rows, values)


def gram_matrix(left, right, weight):
    local_gram = jnp.einsum(
        "gsir,gsic->rc", left * weight[..., None], right, precision=lax.Precision.HIGHEST
    )
    return lax.psum(local_gram, ("group", "sub"))


def spd_solve(matrix, rhs_block):
    factor = jnp.linalg.cholesky(matrix)
    half = lax.linalg.triangular_solve(factor, rhs_block, left_side=True, lower=True)
    return lax.linalg.triangular_solve(factor, half, left_side=True, lower=True, transpose_a=True)


def contract(blocks, mixing):
    return jnp.einsum("gsir,rc->gsic", blocks, mixing, precision=lax.Precision.HIGHEST)


def shards(
    schur, local_inverse, rhs_parts, basis, coarse_map, coarse_inverse, shared_rows, shared_counts
):
    capacity = shared_rows.shape[-1]
    rows_local = rhs_parts.shape[2]
    columns = rhs_parts.shape[3]
    coarse_total = coarse_inverse.shape[2]
    live_mask = (jnp.arange(capacity, dtype=jnp.int32) < shared_counts[..., None]).astype(
        jnp.float32
    )
    own_rows = shared_rows[:, :, 0]
    partner_rows = shared_rows[:, :, 1]
    weight = 1.0 / count_rows(own_rows, live_mask, rows_local)
    selector = (
        coarse_map.reshape(-1)[:, None] == jnp.arange(coarse_total, dtype=jnp.int32)[None, :]
    ).astype(jnp.float32)
    selector_half = selector.astype(jnp.bfloat16)
    full_inverse = coarse_inverse[0]

    def precondition(resid):
        scaled = (weight[..., None] * resid).astype(jnp.bfloat16)
        local_part = jnp.einsum(
            "gsij,gsjr->gsir", local_inverse, scaled, preferred_element_type=jnp.float32
        )
        coarse_local = jnp.einsum(
            "gsmi,gsir->gsmr", basis, scaled, preferred_element_type=jnp.float32
        )
        contrib = jnp.dot(
            selector.T, coarse_local.reshape(-1, columns), precision=lax.Precision.HIGHEST
        )
        coarse_residual = lax.psum(contrib, "sub")
        coarse_rounded = coarse_residual.astype(jnp.bfloat16)
        row_values = jnp.dot(
            full_inverse, coarse_rounded, preferred_element_type=jnp.float32
        ).astype(jnp.bfloat16)
        coarse_values = lax.all_gather(row_values, "sub", axis=0, tiled=True)
        picked = (
            jnp.dot(selector_half, coarse_values, preferred_element_type=jnp.float32)
            .astype(jnp.bfloat16)
            .reshape(coarse_local.shape)
        )
        coarse_part = jnp.einsum(
            "gsmi,gsmr->gsir", basis, picked, preferred_element_type=jnp.float32
        )
        smoothed = weight[..., None] * (local_part + coarse_part)
        return assemble(smoothed, own_rows, partner_rows, live_mask)

    residual = assemble(rhs_parts.astype(jnp.float32), own_rows, partner_rows, live_mask)
    solution = jnp.zeros_like(residual)
    precond = precondition(residual)
    direction = precond
    inner = gram_matrix(precond, residual, weight)
    for iteration in range(ITERS):
        local_image = jnp.einsum(
            "gsij,gsjr->gsir",
            schur,
            direction.astype(jnp.bfloat16),
            preferred_element_type=jnp.float32,
        )
        image = assemble(local_image, own_rows, partner_rows, live_mask)
        curvature = gram_matrix(direction, image, weight)
        step_size = spd_solve(curvature, inner)
        solution = solution + contract(direction, step_size)
        residual = residual - contract(image, step_size)
        if iteration + 1 < ITERS:
            precond = precondition(residual)
            inner_next = gram_matrix(precond, residual, weight)
            conjugacy = spd_solve(inner, inner_next)
            direction = precond + contract(direction, conjugacy)
            inner = inner_next
    return (solution, residual)


def solution(mesh):
    placed = (
        P("group", "sub", None, None),
        P("group", "sub", None, None),
        P("group", "sub", None, None),
        P("group", "sub", None, None),
        P("group", "sub", None),
        P("group", "sub", None),
        P("group", "sub", None, None, None),
        P("group", "sub", None),
    )
    return jax.shard_map(
        shards,
        mesh=mesh,
        in_specs=placed,
        out_specs=(P("group", "sub", None, None), P("group", "sub", None, None)),
        check_vma=False,
    )
```

profile of v0, /device:TPU:1, one launch (start us, length us, event | category | flops | bytes accessed | tf_op | source)
XLA Modules:
  0.0 1686.3 jit_solution(6008829933205526659)
XLA Ops:
  9.2 4.5 collective-permute-start
  20.1 4.4 collective-permute-done.1
  26.9 4.4 collective-permute-start.3
  32.6 7.6 scatter_custom_fusion
  44.1 14.3 collective-permute-done.3
  68.9 6.7 scatter_custom_fusion.1
  78.5 66.6 %all-reduce.19 = bf16[1024,128]{1,0:T(8,128)(2,1)} all-reduce(f32[1024,128]{1,0:T(8,128)S(1)} %fusion.81), channel_id=1, replica_groups=mesh['group'=8,'sub'=16] {'sub'}, use_global_device_ids=true, to_apply=%region_2.0 | all-reduce | flops 131072 | bytes 786432 | tf_op jit(solution)/shard_map/psum | solution.py:106
  146.2 18.0 %all_gather.9 = bf16[1024,128]{1,0:T(8,128)(2,1)} all-gather(bf16[64,128]{1,0:T(8,128)(2,1)S(1)} %fusion.21), channel_id=1, replica_groups=mesh['group'=8,'sub'=16] {'sub'}, dimensions={0}, use_global_device_ids=true | all-gather | bytes 278528 | tf_op jit(solution)/shard_map/all_gather | solution.py:111
  165.8 27.7 %collective-permute-start.4 = (f32[1,1,1024,128]{2,3,1,0:T(8,128)S(1)}, f32[1,1,1024,128]{2,3,1,0:T(8,128)S(1)}, u32[]{:S(2)}, u32[]{:S(2)}) collective-permute-start(f32[1,1,1024,128]{2,3,1,0:T(8,128)S(1)} %bitcast.401), channel_id=1, source_target_pairs={{0,16},{16,32},{32,48},{48,64},{64,80},{80,96},{96,112},{1,17},{17... | collective-permute-start | bytes 1572872 | tf_op jit(solution)/shard_map/ppermute | solution.py:14
  195.5 4.2 collective-permute-done.4
  199.7 4.4 collective-permute-done.5
  205.4 4.6 collective-permute-start.7
  219.2 3.0 gather_fusion.6
  222.3 14.5 collective-permute-done.7
  240.6 3.0 gather_fusion.5
  247.6 3.1 gather_fusion.4
  252.7 6.7 scatter_custom_fusion.2
  261.9 8.1 collective-permute-start.8
  271.9 4.2 collective-permute-done.8
  276.1 4.4 collective-permute-done.9
  281.8 5.7 collective-permute-start.11
  298.6 15.6 collective-permute-done.11
  326.6 7.1 scatter_custom_fusion.3
  335.6 149.4 %all-reduce.18.cloned.1.call-done = (f32[128,128]{0,1:T(8,128)}, f32[128,128]{0,1:T(8,128)}) async-done(((f32[128,128]{0,1:T(8,128)}, f32[128,128]{0,1:T(8,128)}), (f32[128,128]{0,1:T(8,128)}, f32[128,128]{0,1:T(8,128)})) %all-reduce.18.cloned.1.call-update) | async-done | bytes 131088 | tf_op jit(solution)/shard_map/psum | solution.py:63
  488.4 12.5 cholesky.89
  502.3 9.8 custom-call.73
  518.9 64.9 %all-reduce.20 = bf16[1024,128]{1,0:T(8,128)(2,1)} all-reduce(f32[1024,128]{1,0:T(8,128)} %fusion.80), channel_id=1, replica_groups=mesh['group'=8,'sub'=16] {'sub'}, use_global_device_ids=true, to_apply=%region_9.13 | all-reduce | flops 131072 | bytes 786432 | tf_op jit(solution)/shard_map/psum | solution.py:106
  584.9 18.3 %all_gather.10 = bf16[1024,128]{1,0:T(8,128)(2,1)} all-gather(bf16[64,128]{1,0:T(8,128)(2,1)S(1)} %fusion.22), channel_id=1, replica_groups=mesh['group'=8,'sub'=16] {'sub'}, dimensions={0}, use_global_device_ids=true | all-gather | bytes 278528 | tf_op jit(solution)/shard_map/all_gather | solution.py:111
  605.6 21.6 %collective-permute-start.12 = (f32[1,1,1024,128]{2,3,1,0:T(8,128)}, f32[1,1,1024,128]{2,3,1,0:T(8,128)S(1)}, u32[]{:S(2)}, u32[]{:S(2)}) collective-permute-start(f32[1,1,1024,128]{2,3,1,0:T(8,128)} %bitcast.405), channel_id=1, source_target_pairs={{0,16},{16,32},{32,48},{48,64},{64,80},{80,96},{96,112},{1,17},{17... | collective-permute-start | bytes 1572872 | tf_op jit(solution)/shard_map/ppermute | solution.py:14
  629.1 4.5 collective-permute-done.12
  633.6 4.3 collective-permute-done.13
  640.4 4.2 collective-permute-start.15
  647.9 12.5 cholesky.100
  663.2 3.1 gather_fusion.15
  687.6 8.2 scatter_custom_fusion.4
  699.7 9.8 custom-call.75
  709.5 135.7 %all-reduce.10.cloned.1.call-done = f32[128,128]{0,1:T(8,128)} async-done(((f32[128,128]{0,1:T(8,128)}), f32[128,128]{0,1:T(8,128)}) %all-reduce.10.cloned.1.call-update) | async-done | bytes 65552 | tf_op jit(solution)/shard_map/psum | solution.py:63
  854.9 4.2 collective-permute-done.16
  859.1 4.4 collective-permute-done.17
  864.8 4.1 collective-permute-start.19
  874.3 3.1 gather_fusion.19
  882.4 13.5 collective-permute-done.19
  911.8 8.3 scatter_custom_fusion.5
  923.4 144.1 %all-reduce.12.cloned.1.call-done = f32[128,128]{0,1:T(8,128)} async-done(((f32[128,128]{0,1:T(8,128)}), f32[128,128]{0,1:T(8,128)}) %all-reduce.12.cloned.1.call-update) | async-done | bytes 65552 | tf_op jit(solution)/shard_map/psum | solution.py:63
  1070.6 13.2 cholesky.111
  1087.4 11.3 custom-call.77
  1107.0 64.4 %all-reduce.21 = bf16[1024,128]{1,0:T(8,128)(2,1)} all-reduce(f32[1024,128]{1,0:T(8,128)} %fusion.79), channel_id=1, replica_groups=mesh['group'=8,'sub'=16] {'sub'}, use_global_device_ids=true, to_apply=%region_14.18 | all-reduce | flops 131072 | bytes 786432 | tf_op jit(solution)/shard_map/psum | solution.py:106
  1172.4 18.2 %all_gather.11 = bf16[1024,128]{1,0:T(8,128)(2,1)} all-gather(bf16[64,128]{1,0:T(8,128)(2,1)S(1)} %fusion.23), channel_id=1, replica_groups=mesh['group'=8,'sub'=16] {'sub'}, dimensions={0}, use_global_device_ids=true | all-gather | bytes 278528 | tf_op jit(solution)/shard_map/all_gather | solution.py:111
  1193.0 21.2 %collective-permute-start.20 = (f32[1,1,1024,128]{2,3,1,0:T(8,128)}, f32[1,1,1024,128]{2,3,1,0:T(8,128)S(1)}, u32[]{:S(2)}, u32[]{:S(2)}) collective-permute-start(f32[1,1,1024,128]{2,3,1,0:T(8,128)} %bitcast.397), channel_id=1, source_target_pairs={{0,16},{16,32},{32,48},{48,64},{64,80},{80,96},{96,112},{1,17},{17... | collective-permute-start | bytes 1572872 | tf_op jit(solution)/shard_map/ppermute | solution.py:14
  1216.1 4.5 collective-permute-done.20
  1220.6 4.3 collective-permute-done.21
  1227.4 4.2 collective-permute-start.23
  1233.2 11.7 cholesky.122
  1274.6 8.2 scatter_custom_fusion.6
  1286.7 9.8 custom-call.79
  1296.5 134.3 %all-reduce.14.cloned.1.call-done = f32[128,128]{1,0:T(8,128)} async-done(((f32[128,128]{1,0:T(8,128)}), f32[128,128]{1,0:T(8,128)}) %all-reduce.14.cloned.1.call-update) | async-done | bytes 65552 | tf_op jit(solution)/shard_map/psum | solution.py:63
  1440.8 4.2 collective-permute-done.24
  1445.0 4.4 collective-permute-done.25
  1450.7 4.1 collective-permute-start.27
  1464.9 16.9 %collective-permute-done.27 = f32[3,1,1024,128]{2,3,1,0:T(8,128)} collective-permute-done((f32[3,1,1024,128]{2,3,1,0:T(8,128)}, f32[3,1,1024,128]{2,3,1,0:T(8,128)}, u32[]{:S(2)}, u32[]{:S(2)}) %collective-permute-start.27) | collective-permute-done | bytes 1572896 | tf_op jit(solution)/shard_map/ppermute | solution.py:14
  1494.4 8.5 scatter_custom_fusion.7
  1508.2 142.2 %all-reduce.16.cloned.1.call-done = f32[128,128]{0,1:T(8,128)} async-done(((f32[128,128]{0,1:T(8,128)}), f32[128,128]{0,1:T(8,128)}) %all-reduce.16.cloned.1.call-update) | async-done | bytes 65552 | tf_op jit(solution)/shard_map/psum | solution.py:63
  1652.2 11.7 cholesky.133
  1665.2 9.8 custom-call.81
  (281 shorter events, 281.1 us)
Async XLA Ops:
  7.2 68.4 %copy-start = (bf16[1,1,1024,1024]{3,2,1,0:T(8,128)(2,1)S(1)}, bf16[1,1,1024,1024]{3,2,1,0:T(8,128)(2,1)}, u32[]{:S(2)}) copy-start(bf16[1,1,1024,1024]{3,2,1,0:T(8,128)(2,1)} %param.14) | copy-start | bytes 6291460
  7.2 477.8 %all-reduce.18.cloned.1.call-start = ((), (), s32[]{:S(2)}) async-start(), calls=%async_computation.4 | async-start | bytes 262144 | tf_op jit(solution)/shard_map/psum | solution.py:63
  9.2 10.9 collective-permute-start
  13.7 10.8 collective-permute-start.1
  26.9 31.5 %collective-permute-start.3 = (f32[3,1,1024,128]{3,2,1,0:T(8,128)}, f32[3,1,1024,128]{3,2,1,0:T(8,128)}, u32[]{:S(2)}, u32[]{:S(2)}) collective-permute-start(f32[3,1,1024,128]{3,2,1,0:T(8,128)} %pad_maximum_fusion), channel_id=1, source_target_pairs={{0,1},{1,2},{2,3},{3,4},{4,5},{5,6},{6,7},{7,8},{8,9},{9,10},{10,1... | collective-permute-start | bytes 4718600 | tf_op jit(solution)/shard_map/ppermute | solution.py:14
  31.3 32.4 %collective-permute-start.2 = (f32[3,1,1024,128]{3,2,1,0:T(8,128)}, f32[3,1,1024,128]{3,2,1,0:T(8,128)}, u32[]{:S(2)}, u32[]{:S(2)}) collective-permute-start(f32[3,1,1024,128]{3,2,1,0:T(8,128)} %pad_maximum_fusion), channel_id=1, source_target_pairs={{1,0},{2,1},{3,2},{4,3},{5,4},{6,5},{7,6},{8,7},{9,8},{10,9},{11,1... | collective-permute-start | bytes 4718600 | tf_op jit(solution)/shard_map/ppermute | solution.py:17
  75.5 215.2 %copy-start.4 = (f32[1024,128]{1,0:T(8,128)}, f32[1024,128]{1,0:T(8,128)S(1)}, u32[]{:S(2)}) copy-start(f32[1024,128]{1,0:T(8,128)S(1)} %scatter_custom_fusion.1) | copy-start | bytes 1572868
  75.6 1.9 copy-start.14
  75.6 2.2 copy-start.33
  77.4 67.6 %copy-start.28 = (bf16[1,64,1024]{2,1,0:T(8,128)(2,1)S(1)}, bf16[1,64,1024]{2,1,0:T(8,128)(2,1)}, u32[]{:S(2)}) copy-start(bf16[1,64,1024]{2,1,0:T(8,128)(2,1)} %param.18) | copy-start | bytes 393220
  165.8 39.6 %copy-start.10 = (f32[128,1024]{1,0:T(8,128)}, f32[128,1024]{1,0:T(8,128)S(1)}, u32[]{:S(2)}) copy-start(f32[128,1024]{1,0:T(8,128)S(1)} %fusion.12) | copy-start | bytes 1572868
  165.8 33.9 %collective-permute-start.4 = (f32[1,1,1024,128]{2,3,1,0:T(8,128)S(1)}, f32[1,1,1024,128]{2,3,1,0:T(8,128)S(1)}, u32[]{:S(2)}, u32[]{:S(2)}) collective-permute-start(f32[1,1,1024,128]{2,3,1,0:T(8,128)S(1)} %bitcast.401), channel_id=1, source_target_pairs={{0,16},{16,32},{32,48},{48,64},{64,80},{80,96},{96,112},{1,17},{17... | collective-permute-start | bytes 1572872 | tf_op jit(solution)/shard_map/ppermute | solution.py:14
  193.6 10.5 collective-permute-start.5
  199.7 5.7 copy-start.24
  205.4 31.3 %collective-permute-start.7 = (f32[3,1,1024,128]{2,3,1,0:T(8,128)}, f32[3,1,1024,128]{2,3,1,0:T(8,128)}, u32[]{:S(2)}, u32[]{:S(2)}) collective-permute-start(f32[3,1,1024,128]{2,3,1,0:T(8,128)} %pad_maximum_fusion.1), channel_id=1, source_target_pairs={{0,1},{1,2},{2,3},{3,4},{4,5},{5,6},{6,7},{7,8},{8,9},{9,10},{10,1... | collective-permute-start | bytes 4718600 | tf_op jit(solution)/shard_map/ppermute | solution.py:14
  210.0 33.7 %collective-permute-start.6 = (f32[3,1,1024,128]{2,3,1,0:T(8,128)}, f32[3,1,1024,128]{2,3,1,0:T(8,128)}, u32[]{:S(2)}, u32[]{:S(2)}) collective-permute-start(f32[3,1,1024,128]{2,3,1,0:T(8,128)} %pad_maximum_fusion.1), channel_id=1, source_target_pairs={{1,0},{2,1},{3,2},{4,3},{5,4},{6,5},{7,6},{8,7},{9,8},{10,9},{11,1... | collective-permute-start | bytes 4718600 | tf_op jit(solution)/shard_map/ppermute | solution.py:17
  261.8 20.0 %copy-start.12 = (f32[128,1024]{1,0:T(8,128)}, f32[128,1024]{1,0:T(8,128)S(1)}, u32[]{:S(2)}) copy-start(f32[128,1024]{1,0:T(8,128)S(1)} %fusion.4) | copy-start | bytes 1572868
  261.9 14.2 collective-permute-start.8
  269.9 10.5 collective-permute-start.9
  276.1 5.7 copy-start.22
  280.4 1.4 copy-start.23
  281.8 32.4 %collective-permute-start.11 = (f32[3,1,1024,128]{2,3,1,0:T(8,128)}, f32[3,1,1024,128]{2,3,1,0:T(8,128)}, u32[]{:S(2)}, u32[]{:S(2)}) collective-permute-start(f32[3,1,1024,128]{2,3,1,0:T(8,128)} %pad_maximum_fusion.2), channel_id=1, source_target_pairs={{0,1},{1,2},{2,3},{3,4},{4,5},{5,6},{6,7},{7,8},{8,9},{9,10},{10,1... | collective-permute-start | bytes 4718600 | tf_op jit(solution)/shard_map/ppermute | solution.py:14
  287.5 32.0 %collective-permute-start.10 = (f32[3,1,1024,128]{2,3,1,0:T(8,128)}, f32[3,1,1024,128]{2,3,1,0:T(8,128)}, u32[]{:S(2)}, u32[]{:S(2)}) collective-permute-start(f32[3,1,1024,128]{2,3,1,0:T(8,128)} %pad_maximum_fusion.2), channel_id=1, source_target_pairs={{1,0},{2,1},{3,2},{4,3},{5,4},{6,5},{7,6},{8,7},{9,8},{10,9},{11,1... | collective-permute-start | bytes 4718600 | tf_op jit(solution)/shard_map/ppermute | solution.py:17
  321.5 5.1 copy-start.8
  333.7 179.5 %copy-start.9 = (f32[1024,128]{1,0:T(8,128)}, f32[1024,128]{1,0:T(8,128)S(1)}, u32[]{:S(2)}) copy-start(f32[1024,128]{1,0:T(8,128)S(1)} %scatter_custom_fusion.3) | copy-start | bytes 1572868
  335.5 509.6 %all-reduce.10.cloned.1.call-start = ((), (), s32[]{:S(2)}) async-start(), calls=%async_computation | async-start | bytes 131072 | tf_op jit(solution)/shard_map/psum | solution.py:63
  515.2 180.6 %copy-start.3 = (f32[1,1,1024,128]{3,2,1,0:T(8,128)}, f32[1,1,1024,128]{3,2,1,0:T(8,128)S(1)}, u32[]{:S(2)}) copy-start(f32[1,1,1024,128]{3,2,1,0:T(8,128)S(1)} %fusion.16) | copy-start | bytes 1572868
  605.6 28.0 %collective-permute-start.12 = (f32[1,1,1024,128]{2,3,1,0:T(8,128)}, f32[1,1,1024,128]{2,3,1,0:T(8,128)S(1)}, u32[]{:S(2)}, u32[]{:S(2)}) collective-permute-start(f32[1,1,1024,128]{2,3,1,0:T(8,128)} %bitcast.405), channel_id=1, source_target_pairs={{0,16},{16,32},{32,48},{48,64},{64,80},{80,96},{96,112},{1,17},{17... | collective-permute-start | bytes 1572872 | tf_op jit(solution)/shard_map/ppermute | solution.py:14
  627.1 10.7 collective-permute-start.13
  633.6 6.8 copy-start.18
  637.9 2.5 copy-start.19
  640.4 31.3 %collective-permute-start.15 = (f32[3,1,1024,128]{2,3,1,0:T(8,128)}, f32[3,1,1024,128]{2,3,1,0:T(8,128)}, u32[]{:S(2)}, u32[]{:S(2)}) collective-permute-start(f32[3,1,1024,128]{2,3,1,0:T(8,128)} %pad_maximum_fusion.3), channel_id=1, source_target_pairs={{0,1},{1,2},{2,3},{3,4},{4,5},{5,6},{6,7},{7,8},{8,9},{9,10},{10,1... | collective-permute-start | bytes 4718600 | tf_op jit(solution)/shard_map/ppermute | solution.py:14
  644.6 34.0 %collective-permute-start.14 = (f32[3,1,1024,128]{2,3,1,0:T(8,128)}, f32[3,1,1024,128]{2,3,1,0:T(8,128)}, u32[]{:S(2)}, u32[]{:S(2)}) collective-permute-start(f32[3,1,1024,128]{2,3,1,0:T(8,128)} %pad_maximum_fusion.3), channel_id=1, source_target_pairs={{1,0},{2,1},{3,2},{4,3},{5,4},{6,5},{7,6},{8,7},{9,8},{10,9},{11,1... | collective-permute-start | bytes 4718600 | tf_op jit(solution)/shard_map/ppermute | solution.py:17
  698.7 368.8 %all-reduce.12.cloned.1.call-start = ((), (), s32[]{:S(2)}) async-start(), calls=%async_computation.1 | async-start | bytes 131072 | tf_op jit(solution)/shard_map/psum | solution.py:63
  850.5 14.3 copy-start.13
  850.5 8.5 collective-permute-start.16
  853.0 10.5 collective-permute-start.17
  859.1 5.7 copy-start.26
  864.8 31.1 %collective-permute-start.19 = (f32[3,1,1024,128]{2,3,1,0:T(8,128)}, f32[3,1,1024,128]{2,3,1,0:T(8,128)}, u32[]{:S(2)}, u32[]{:S(2)}) collective-permute-start(f32[3,1,1024,128]{2,3,1,0:T(8,128)} %pad_maximum_fusion.4), channel_id=1, source_target_pairs={{0,1},{1,2},{2,3},{3,4},{4,5},{5,6},{6,7},{7,8},{8,9},{9,10},{10,1... | collective-permute-start | bytes 4718600 | tf_op jit(solution)/shard_map/ppermute | solution.py:14
  868.9 33.9 %collective-permute-start.18 = (f32[3,1,1024,128]{2,3,1,0:T(8,128)}, f32[3,1,1024,128]{2,3,1,0:T(8,128)}, u32[]{:S(2)}, u32[]{:S(2)}) collective-permute-start(f32[3,1,1024,128]{2,3,1,0:T(8,128)} %pad_maximum_fusion.4), channel_id=1, source_target_pairs={{1,0},{2,1},{3,2},{4,3},{5,4},{6,5},{7,6},{8,7},{9,8},{10,9},{11,1... | collective-permute-start | bytes 4718600 | tf_op jit(solution)/shard_map/ppermute | solution.py:17
  911.8 186.9 %copy-start.29 = (f32[128,128]{0,1:T(8,128)S(1)}, f32[128,128]{0,1:T(8,128)}, u32[]{:S(2)}) copy-start(f32[128,128]{0,1:T(8,128)} %all-reduce.10.cloned.1.call-done) | copy-start | bytes 196612
  922.9 507.9 %all-reduce.14.cloned.1.call-start = ((), (), s32[]{:S(2)}) async-start(), calls=%async_computation.2 | async-start | bytes 131072 | tf_op jit(solution)/shard_map/psum | solution.py:63
  1103.3 1.9 copy-start.1
  1193.0 27.6 %collective-permute-start.20 = (f32[1,1,1024,128]{2,3,1,0:T(8,128)}, f32[1,1,1024,128]{2,3,1,0:T(8,128)S(1)}, u32[]{:S(2)}, u32[]{:S(2)}) collective-permute-start(f32[1,1,1024,128]{2,3,1,0:T(8,128)} %bitcast.397), channel_id=1, source_target_pairs={{0,16},{16,32},{32,48},{48,64},{64,80},{80,96},{96,112},{1,17},{17... | collective-permute-start | bytes 1572872 | tf_op jit(solution)/shard_map/ppermute | solution.py:14
  1214.2 10.7 collective-permute-start.21
  1220.6 6.8 copy-start.16
  1224.9 2.5 copy-start.17
  1227.4 31.3 %collective-permute-start.23 = (f32[3,1,1024,128]{2,3,1,0:T(8,128)}, f32[3,1,1024,128]{2,3,1,0:T(8,128)}, u32[]{:S(2)}, u32[]{:S(2)}) collective-permute-start(f32[3,1,1024,128]{2,3,1,0:T(8,128)} %pad_maximum_fusion.5), channel_id=1, source_target_pairs={{0,1},{1,2},{2,3},{3,4},{4,5},{5,6},{6,7},{7,8},{8,9},{9,10},{10,1... | collective-permute-start | bytes 4718600 | tf_op jit(solution)/shard_map/ppermute | solution.py:14
  1231.6 34.0 %collective-permute-start.22 = (f32[3,1,1024,128]{2,3,1,0:T(8,128)}, f32[3,1,1024,128]{2,3,1,0:T(8,128)}, u32[]{:S(2)}, u32[]{:S(2)}) collective-permute-start(f32[3,1,1024,128]{2,3,1,0:T(8,128)} %pad_maximum_fusion.5), channel_id=1, source_target_pairs={{1,0},{2,1},{3,2},{4,3},{5,4},{6,5},{7,6},{8,7},{9,8},{10,9},{11,1... | collective-permute-start | bytes 4718600 | tf_op jit(solution)/shard_map/ppermute | solution.py:17
  1285.8 364.6 %all-reduce.16.cloned.1.call-start = ((), (), s32[]{:S(2)}) async-start(), calls=%async_computation.3 | async-start | bytes 131072 | tf_op jit(solution)/shard_map/psum | solution.py:63
  1433.8 2.6 copy-start.5
  1436.4 14.3 copy-start.11
  1436.4 8.5 collective-permute-start.24
  1438.9 10.5 collective-permute-start.25
  1445.0 5.8 copy-start.21
  1449.4 1.4 copy-start.20
  1450.7 31.1 %collective-permute-start.27 = (f32[3,1,1024,128]{2,3,1,0:T(8,128)}, f32[3,1,1024,128]{2,3,1,0:T(8,128)}, u32[]{:S(2)}, u32[]{:S(2)}) collective-permute-start(f32[3,1,1024,128]{2,3,1,0:T(8,128)} %pad_maximum_fusion.6), channel_id=1, source_target_pairs={{0,1},{1,2},{2,3},{3,4},{4,5},{5,6},{6,7},{7,8},{8,9},{9,10},{10,1... | collective-permute-start | bytes 4718600 | tf_op jit(solution)/shard_map/ppermute | solution.py:14
  1454.9 32.2 %collective-permute-start.26 = (f32[3,1,1024,128]{2,3,1,0:T(8,128)}, f32[3,1,1024,128]{2,3,1,0:T(8,128)}, u32[]{:S(2)}, u32[]{:S(2)}) collective-permute-start(f32[3,1,1024,128]{2,3,1,0:T(8,128)} %pad_maximum_fusion.6), channel_id=1, source_target_pairs={{1,0},{2,1},{3,2},{4,3},{5,4},{6,5},{7,6},{8,7},{9,8},{10,9},{11,1... | collective-permute-start | bytes 4718600 | tf_op jit(solution)/shard_map/ppermute | solution.py:17
  1492.3 10.6 copy-start.6
  1493.4 12.4 copy-start.31
  1502.9 172.2 %copy-start.32 = (f32[128,128]{1,0:T(8,128)S(1)}, f32[128,128]{1,0:T(8,128)}, u32[]{:S(2)}) copy-start(f32[128,128]{1,0:T(8,128)} %all-reduce.14.cloned.1.call-done) | copy-start | bytes 196612
  1505.7 169.8 %copy-start.2 = (f32[1,1,1024,128]{3,2,1,0:T(8,128)S(1)}, f32[1,1,1024,128]{3,2,1,0:T(8,128)}, u32[]{:S(2)}) copy-start(f32[1,1,1024,128]{3,2,1,0:T(8,128)} %copy-done.1) | copy-start | bytes 1572868
  1508.2 169.8 %copy-start.7 = (f32[1,1,1024,128]{3,2,1,0:T(8,128)S(1)}, f32[1,1,1024,128]{3,2,1,0:T(8,128)}, u32[]{:S(2)}) copy-start(f32[1,1,1024,128]{3,2,1,0:T(8,128)} %copy-done.5) | copy-start | bytes 1572868
  1675.0 2.9 copy-start.15
  (3 other events, 3.3 us)
Sparse Core Ops, SparseCore 0:
  335.7 149.2 all-reduce.17
  698.8 146.3 all-reduce.9
  923.0 144.4 all-reduce.11
  1285.9 144.8 all-reduce.13
  1505.9 144.4 all-reduce.15
where the time goes:
time: 1700 us; the launch traced here: 1690 us
  waiting for transfers between devices  842 us (50%)
  blocking collectives  250 us (15%)
  other arithmetic  218 us (13%)
  local copies, waits for them, and re-layouts  155 us (9%)
  starting transfers between devices  143 us (8%)
  matrix products  63.4 us (4%)
    psum x5, waiting for transfers between devices, gram_matrix(): return lax.psum(local_gram, ('group', 'sub'))  706 us
    psum x3, blocking collectives, precondition(): coarse_residual = lax.psum(contrib, 'sub')  196 us
    ppermute x14, starting transfers between devices, extended(): lax.ppermute(lax.slice_in_dim(block, block.shape[dim] - width, None, axis...  119 us
    ppermute x14, waiting for transfers between devices, extended(): lax.ppermute(lax.slice_in_dim(block, block.shape[dim] - width, None, axis...  103 us
    gather x28, local copies, waits for them, and re-layouts, pick_rows(): source_block[rows_at]  70.6 us
    another operation x15, other arithmetic, spd_solve(): factor = jnp.linalg.cholesky(matrix)  66 us
    another operation x10, other arithmetic, spd_solve(): lax.linalg.triangular_solve(factor, half, left_side=True, lower=True, tra...  55.3 us
    all_gather x3, blocking collectives, precondition(): coarse_values = lax.all_gather(row_values, 'sub', axis=0, tiled=True)  54.4 us
  transfers between devices with their start and end apart: 33, of which 27 were waited for; matrix products, arithmetic and copies ran while one was open for 10% of the time, Pallas kernels for 0%

commit v1 on v0

--- a/solution.py
+++ b/solution.py
@@ -60,7 +60,7 @@
     local_gram = jnp.einsum(
         "gsir,gsic->rc", left * weight[..., None], right, precision=lax.Precision.HIGHEST
     )
-    return lax.psum(local_gram, ("group", "sub"))
+    return jnp.sum(lax.all_gather(local_gram, ("group", "sub")), axis=0)
 
 
 def spd_solve(matrix, rhs_block):

time: 1700 us -> 1380 us (0.81)
  waiting for transfers between devices: 842 us -> 503 us
    psum x5 -> x0, waiting for transfers between devices: 706 us -> none  [gram_matrix(): return lax.psum(local_gram, ('group', 'sub'))]
    all_gather x0 -> x6, waiting for transfers between devices: none -> 348 us  [gram_matrix(): return jnp.sum(lax.all_gather(local_gram, ('group', 'sub')), axis=0)]
    reduce_sum x0 -> x6, other arithmetic: none -> 22.9 us  [gram_matrix(): return jnp.sum(lax.all_gather(local_gram, ('group', 'sub')), axis=0)]
    ppermute x14, waiting for transfers between devices: 103 us -> 122 us  [extended(): lax.ppermute(lax.slice_in_dim(block, block.shape[dim] - width, None, axis...]
  transfers between devices with their start and end apart: 33 -> 34, of which waited for: 27 -> 28; matrix products, arithmetic and copies ran while one was open for 10% -> 15% of each run, Pallas kernels for 0% -> 0%
where the time goes in v1:
time: 1380 us; the launch traced here: 1370 us
  waiting for transfers between devices  503 us (36%)
  blocking collectives  250 us (18%)
  other arithmetic  234 us (17%)
  local copies, waits for them, and re-layouts  167 us (12%)
  starting transfers between devices  142 us (10%)
  matrix products  58.3 us (4%)
  between operations  15.6 us (1%)
    all_gather x6, waiting for transfers between devices, gram_matrix(): return jnp.sum(lax.all_gather(local_gram, ('group', 'sub')), axis=0)  348 us
    psum x3, blocking collectives, precondition(): coarse_residual = lax.psum(contrib, 'sub')  196 us
    ppermute x14, waiting for transfers between devices, extended(): lax.ppermute(lax.slice_in_dim(block, block.shape[dim] - width, None, axis...  122 us
    ppermute x14, starting transfers between devices, extended(): lax.ppermute(lax.slice_in_dim(block, block.shape[dim] - width, None, axis...  117 us
    gather x28, local copies, waits for them, and re-layouts, pick_rows(): source_block[rows_at]  79.1 us
    another operation x15, other arithmetic, spd_solve(): factor = jnp.linalg.cholesky(matrix)  62.9 us
    all_gather x3, blocking collectives, precondition(): coarse_values = lax.all_gather(row_values, 'sub', axis=0, tiled=True)  54.5 us
    another operation x10, other arithmetic, spd_solve(): lax.linalg.triangular_solve(factor, half, left_side=True, lower=True, tra...  53.8 us
  transfers between devices with their start and end apart: 34, of which 28 were waited for; matrix products, arithmetic and copies ran while one was open for 15% of the time, Pallas kernels for 0%

profile of v1, /device:TPU:1, one launch (start us, length us, event | category | flops | bytes accessed | tf_op | source)
XLA Modules:
  0.0 1371.2 jit_solution(5008210219202996138)
XLA Ops:
  9.2 4.5 collective-permute-start
  20.1 4.4 collective-permute-done.1
  26.9 4.3 collective-permute-start.3
  32.6 7.6 scatter_custom_fusion
  44.1 14.4 %collective-permute-done.3 = f32[3,1,1024,128]{3,2,1,0:T(8,128)} collective-permute-done((f32[3,1,1024,128]{3,2,1,0:T(8,128)}, f32[3,1,1024,128]{3,2,1,0:T(8,128)}, u32[]{:S(2)}, u32[]{:S(2)}) %collective-permute-start.3) | collective-permute-done | bytes 1572896 | tf_op jit(solution)/shard_map/ppermute | solution.py:14
  68.8 6.7 scatter_custom_fusion.1
  78.4 66.6 %all-reduce.3 = bf16[1024,128]{1,0:T(8,128)(2,1)} all-reduce(f32[1024,128]{1,0:T(8,128)S(1)} %fusion.81), channel_id=1, replica_groups=mesh['group'=8,'sub'=16] {'sub'}, use_global_device_ids=true, to_apply=%region_2.0 | all-reduce | flops 131072 | bytes 786432 | tf_op jit(solution)/shard_map/psum | solution.py:106
  146.2 18.0 %all_gather.45 = bf16[1024,128]{1,0:T(8,128)(2,1)} all-gather(bf16[64,128]{1,0:T(8,128)(2,1)S(1)} %fusion.21), channel_id=1, replica_groups=mesh['group'=8,'sub'=16] {'sub'}, dimensions={0}, use_global_device_ids=true | all-gather | bytes 278528 | tf_op jit(solution)/shard_map/all_gather | solution.py:111
  165.8 27.8 %collective-permute-start.4 = (f32[1,1,1024,128]{2,3,1,0:T(8,128)S(1)}, f32[1,1,1024,128]{2,3,1,0:T(8,128)S(1)}, u32[]{:S(2)}, u32[]{:S(2)}) collective-permute-start(f32[1,1,1024,128]{2,3,1,0:T(8,128)S(1)} %bitcast.409), channel_id=1, source_target_pairs={{0,16},{16,32},{32,48},{48,64},{64,80},{80,96},{96,112},{1,17},{17... | collective-permute-start | bytes 1572872 | tf_op jit(solution)/shard_map/ppermute | solution.py:14
  195.5 4.2 collective-permute-done.4
  199.7 4.4 collective-permute-done.5
  205.4 4.6 collective-permute-start.7
  222.9 13.8 %collective-permute-done.7 = f32[3,1,1024,128]{2,3,1,0:T(8,128)} collective-permute-done((f32[3,1,1024,128]{2,3,1,0:T(8,128)}, f32[3,1,1024,128]{2,3,1,0:T(8,128)}, u32[]{:S(2)}, u32[]{:S(2)}) %collective-permute-start.7) | collective-permute-done | bytes 1572896 | tf_op jit(solution)/shard_map/ppermute | solution.py:14
  252.8 6.7 scatter_custom_fusion.2
  263.7 8.1 collective-permute-start.8
  273.8 4.3 collective-permute-done.8
  278.1 4.5 collective-permute-done.9
  284.0 5.8 collective-permute-start.11
  302.5 14.0 %collective-permute-done.11 = f32[3,1,1024,128]{2,3,1,0:T(8,128)} collective-permute-done((f32[3,1,1024,128]{2,3,1,0:T(8,128)}, f32[3,1,1024,128]{2,3,1,0:T(8,128)}, u32[]{:S(2)}, u32[]{:S(2)}) %collective-permute-start.11) | collective-permute-done | bytes 1572896 | tf_op jit(solution)/shard_map/ppermute | solution.py:14
  332.6 7.1 scatter_custom_fusion.3
  341.5 24.0 %all-gather.15.cloned.1.call-done = f32[16384,128]{1,0:T(8,128)} async-done(((f32[128,128]{1,0:T(8,128)}), f32[16384,128]{1,0:T(8,128)}) %all-gather.15.cloned.1.call-update) | async-done | bytes 8388624 | tf_op jit(solution)/shard_map/all_gather | solution.py:63
  365.6 3.8 reduce_sum.55
  369.4 67.1 %all-gather.13.cloned.1.call-done = f32[16384,128]{1,0:T(8,128)} async-done(((f32[128,128]{1,0:T(8,128)}), f32[16384,128]{1,0:T(8,128)}) %all-gather.13.cloned.1.call-update) | async-done | bytes 8388624 | tf_op jit(solution)/shard_map/all_gather | solution.py:63
  436.5 3.8 reduce_sum.54
  440.4 11.7 cholesky.89
  453.5 9.8 custom-call.73
  469.8 64.3 %all-reduce.4 = bf16[1024,128]{1,0:T(8,128)(2,1)} all-reduce(f32[1024,128]{1,0:T(8,128)} %fusion.80), channel_id=1, replica_groups=mesh['group'=8,'sub'=16] {'sub'}, use_global_device_ids=true, to_apply=%region_9.13 | all-reduce | flops 131072 | bytes 786432 | tf_op jit(solution)/shard_map/psum | solution.py:106
  535.3 18.1 %all_gather.50 = bf16[1024,128]{1,0:T(8,128)(2,1)} all-gather(bf16[64,128]{1,0:T(8,128)(2,1)S(1)} %fusion.22), channel_id=1, replica_groups=mesh['group'=8,'sub'=16] {'sub'}, dimensions={0}, use_global_device_ids=true | all-gather | bytes 278528 | tf_op jit(solution)/shard_map/all_gather | solution.py:111
  555.8 21.3 %collective-permute-start.12 = (f32[1,1,1024,128]{2,3,1,0:T(8,128)}, f32[1,1,1024,128]{2,3,1,0:T(8,128)S(1)}, u32[]{:S(2)}, u32[]{:S(2)}) collective-permute-start(f32[1,1,1024,128]{2,3,1,0:T(8,128)} %bitcast.413), channel_id=1, source_target_pairs={{0,16},{16,32},{32,48},{48,64},{64,80},{80,96},{96,112},{1,17},{17... | collective-permute-start | bytes 1572872 | tf_op jit(solution)/shard_map/ppermute | solution.py:14
  579.1 4.5 collective-permute-done.12
  583.6 4.3 collective-permute-done.13
  590.4 4.2 collective-permute-start.15
  608.2 13.5 collective-permute-done.15
  637.6 8.2 scatter_custom_fusion.4
  649.1 11.7 cholesky.100
  662.2 9.8 custom-call.75
  672.0 53.4 %all-gather.17.cloned.1.call-done = f32[16384,128]{1,0:T(8,128)} async-done(((f32[128,128]{1,0:T(8,128)}), f32[16384,128]{1,0:T(8,128)}) %all-gather.17.cloned.1.call-update) | async-done | bytes 8388624 | tf_op jit(solution)/shard_map/all_gather | solution.py:63
  725.4 3.8 reduce_sum.56
  741.9 4.4 collective-permute-done.17
  765.1 13.0 collective-permute-done.19
  794.0 8.2 scatter_custom_fusion.5
  805.6 75.9 %all-gather.19.cloned.1.call-done = f32[16384,128]{1,0:T(8,128)} async-done(((f32[128,128]{1,0:T(8,128)}), f32[16384,128]{1,0:T(8,128)}) %all-gather.19.cloned.1.call-update) | async-done | bytes 8388624 | tf_op jit(solution)/shard_map/all_gather | solution.py:63
  881.5 3.8 reduce_sum.57
  887.5 12.5 cholesky.111
  902.1 10.6 custom-call.77
  920.2 64.6 %all-reduce.5 = bf16[1024,128]{1,0:T(8,128)(2,1)} all-reduce(f32[1024,128]{1,0:T(8,128)} %fusion.79), channel_id=1, replica_groups=mesh['group'=8,'sub'=16] {'sub'}, use_global_device_ids=true, to_apply=%region_14.18 | all-reduce | flops 131072 | bytes 786432 | tf_op jit(solution)/shard_map/psum | solution.py:106
  985.9 18.4 %all_gather.55 = bf16[1024,128]{1,0:T(8,128)(2,1)} all-gather(bf16[64,128]{1,0:T(8,128)(2,1)S(1)} %fusion.23), channel_id=1, replica_groups=mesh['group'=8,'sub'=16] {'sub'}, dimensions={0}, use_global_device_ids=true | all-gather | bytes 278528 | tf_op jit(solution)/shard_map/all_gather | solution.py:111
  1006.7 20.8 %collective-permute-start.20 = (f32[1,1,1024,128]{2,3,1,0:T(8,128)}, f32[1,1,1024,128]{2,3,1,0:T(8,128)S(1)}, u32[]{:S(2)}, u32[]{:S(2)}) collective-permute-start(f32[1,1,1024,128]{2,3,1,0:T(8,128)} %bitcast.417), channel_id=1, source_target_pairs={{0,16},{16,32},{32,48},{48,64},{64,80},{80,96},{96,112},{1,17},{17... | collective-permute-start | bytes 1572872 | tf_op jit(solution)/shard_map/ppermute | solution.py:14
  1029.4 4.5 collective-permute-done.20
  1033.9 4.3 collective-permute-done.21
  1040.7 4.2 collective-permute-start.23
  1058.0 14.1 %collective-permute-done.23 = f32[3,1,1024,128]{2,3,1,0:T(8,128)} collective-permute-done((f32[3,1,1024,128]{2,3,1,0:T(8,128)}, f32[3,1,1024,128]{2,3,1,0:T(8,128)}, u32[]{:S(2)}, u32[]{:S(2)}) %collective-permute-start.23) | collective-permute-done | bytes 1572896 | tf_op jit(solution)/shard_map/ppermute | solution.py:14
  1087.9 8.3 scatter_custom_fusion.6
  1099.5 11.7 cholesky.122
  1112.6 9.8 custom-call.79
  1122.4 53.3 %all-gather.21.cloned.1.call-done = f32[16384,128]{1,0:T(8,128)} async-done(((f32[128,128]{1,0:T(8,128)}), f32[16384,128]{1,0:T(8,128)}) %all-gather.21.cloned.1.call-update) | async-done | bytes 8388624 | tf_op jit(solution)/shard_map/all_gather | solution.py:63
  1175.8 3.8 reduce_sum.58
  1192.5 4.4 collective-permute-done.25
  1215.2 13.6 collective-permute-done.27
  1244.6 8.6 scatter_custom_fusion.7
  1258.1 74.5 %all-gather.23.cloned.1.call-done = f32[16384,128]{1,0:T(8,128)} async-done(((f32[128,128]{1,0:T(8,128)}), f32[16384,128]{1,0:T(8,128)}) %all-gather.23.cloned.1.call-update) | async-done | bytes 8388624 | tf_op jit(solution)/shard_map/all_gather | solution.py:63
  1332.6 3.9 reduce_sum.59
  1336.6 11.7 cholesky.133
  1349.8 9.8 custom-call.81
  (285 shorter events, 313.8 us)
Async XLA Ops:
  7.2 68.3 %copy-start = (bf16[1,1,1024,1024]{3,2,1,0:T(8,128)(2,1)S(1)}, bf16[1,1,1024,1024]{3,2,1,0:T(8,128)(2,1)}, u32[]{:S(2)}) copy-start(bf16[1,1,1024,1024]{3,2,1,0:T(8,128)(2,1)} %param.14) | copy-start | bytes 6291460
  7.2 358.4 %all-gather.15.cloned.1.call-start = ((), (), s32[]{:S(2)}) async-start(), calls=%async_computation.1 | async-start | bytes 8454144 | tf_op jit(solution)/shard_map/all_gather | solution.py:63
  9.2 10.9 collective-permute-start
  13.7 10.8 collective-permute-start.1
  26.9 31.5 %collective-permute-start.3 = (f32[3,1,1024,128]{3,2,1,0:T(8,128)}, f32[3,1,1024,128]{3,2,1,0:T(8,128)}, u32[]{:S(2)}, u32[]{:S(2)}) collective-permute-start(f32[3,1,1024,128]{3,2,1,0:T(8,128)} %pad_maximum_fusion), channel_id=1, source_target_pairs={{0,1},{1,2},{2,3},{3,4},{4,5},{5,6},{6,7},{7,8},{8,9},{9,10},{10,1... | collective-permute-start | bytes 4718600 | tf_op jit(solution)/shard_map/ppermute | solution.py:14
  31.3 32.4 %collective-permute-start.2 = (f32[3,1,1024,128]{3,2,1,0:T(8,128)}, f32[3,1,1024,128]{3,2,1,0:T(8,128)}, u32[]{:S(2)}, u32[]{:S(2)}) collective-permute-start(f32[3,1,1024,128]{3,2,1,0:T(8,128)} %pad_maximum_fusion), channel_id=1, source_target_pairs={{1,0},{2,1},{3,2},{4,3},{5,4},{6,5},{7,6},{8,7},{9,8},{10,9},{11,1... | collective-permute-start | bytes 4718600 | tf_op jit(solution)/shard_map/ppermute | solution.py:17
  75.5 183.9 %copy-start.4 = (f32[1024,128]{1,0:T(8,128)}, f32[1024,128]{1,0:T(8,128)S(1)}, u32[]{:S(2)}) copy-start(f32[1024,128]{1,0:T(8,128)S(1)} %scatter_custom_fusion.1) | copy-start | bytes 1572868
  75.5 1.9 copy-start.12
  75.5 2.2 copy-start.30
  77.4 67.6 %copy-start.26 = (bf16[1,64,1024]{2,1,0:T(8,128)(2,1)S(1)}, bf16[1,64,1024]{2,1,0:T(8,128)(2,1)}, u32[]{:S(2)}) copy-start(bf16[1,64,1024]{2,1,0:T(8,128)(2,1)} %param.18) | copy-start | bytes 393220
  165.8 39.6 %copy-start.8 = (f32[128,1024]{1,0:T(8,128)}, f32[128,1024]{1,0:T(8,128)S(1)}, u32[]{:S(2)}) copy-start(f32[128,1024]{1,0:T(8,128)S(1)} %fusion.12) | copy-start | bytes 1572868
  165.8 33.9 %collective-permute-start.4 = (f32[1,1,1024,128]{2,3,1,0:T(8,128)S(1)}, f32[1,1,1024,128]{2,3,1,0:T(8,128)S(1)}, u32[]{:S(2)}, u32[]{:S(2)}) collective-permute-start(f32[1,1,1024,128]{2,3,1,0:T(8,128)S(1)} %bitcast.409), channel_id=1, source_target_pairs={{0,16},{16,32},{32,48},{48,64},{64,80},{80,96},{96,112},{1,17},{17... | collective-permute-start | bytes 1572872 | tf_op jit(solution)/shard_map/ppermute | solution.py:14
  193.5 10.5 collective-permute-start.5
  199.6 11.8 copy-start.15
  204.0 7.4 copy-start.16
  205.4 31.3 %collective-permute-start.7 = (f32[3,1,1024,128]{2,3,1,0:T(8,128)}, f32[3,1,1024,128]{2,3,1,0:T(8,128)}, u32[]{:S(2)}, u32[]{:S(2)}) collective-permute-start(f32[3,1,1024,128]{2,3,1,0:T(8,128)} %pad_maximum_fusion.1), channel_id=1, source_target_pairs={{0,1},{1,2},{2,3},{3,4},{4,5},{5,6},{6,7},{7,8},{8,9},{9,10},{10,1... | collective-permute-start | bytes 4718600 | tf_op jit(solution)/shard_map/ppermute | solution.py:14
  209.9 33.7 %collective-permute-start.6 = (f32[3,1,1024,128]{2,3,1,0:T(8,128)}, f32[3,1,1024,128]{2,3,1,0:T(8,128)}, u32[]{:S(2)}, u32[]{:S(2)}) collective-permute-start(f32[3,1,1024,128]{2,3,1,0:T(8,128)} %pad_maximum_fusion.1), channel_id=1, source_target_pairs={{1,0},{2,1},{3,2},{4,3},{5,4},{6,5},{7,6},{8,7},{9,8},{10,9},{11,1... | collective-permute-start | bytes 4718600 | tf_op jit(solution)/shard_map/ppermute | solution.py:17
  261.3 175.2 %all-gather.13.cloned.1.call-start = ((), (), s32[]{:S(2)}) async-start(), calls=%async_computation | async-start | bytes 8454144 | tf_op jit(solution)/shard_map/all_gather | solution.py:63
  263.7 20.3 %copy-start.9 = (f32[128,1024]{1,0:T(8,128)}, f32[128,1024]{1,0:T(8,128)S(1)}, u32[]{:S(2)}) copy-start(f32[128,1024]{1,0:T(8,128)S(1)} %fusion.4) | copy-start | bytes 1572868
  263.7 14.3 %collective-permute-start.8 = (f32[1,1,1024,128]{2,3,1,0:T(8,128)S(1)}, f32[1,1,1024,128]{2,3,1,0:T(8,128)S(1)}, u32[]{:S(2)}, u32[]{:S(2)}) collective-permute-start(f32[1,1,1024,128]{2,3,1,0:T(8,128)S(1)} %bitcast.421), channel_id=1, source_target_pairs={{0,16},{16,32},{32,48},{48,64},{64,80},{80,96},{96,112},{1,17},{17... | collective-permute-start | bytes 1572872 | tf_op jit(solution)/shard_map/ppermute | solution.py:14
  271.8 10.8 collective-permute-start.9
  278.1 5.9 copy-start.17
  282.6 1.4 copy-start.18
  284.0 32.5 %collective-permute-start.11 = (f32[3,1,1024,128]{2,3,1,0:T(8,128)}, f32[3,1,1024,128]{2,3,1,0:T(8,128)}, u32[]{:S(2)}, u32[]{:S(2)}) collective-permute-start(f32[3,1,1024,128]{2,3,1,0:T(8,128)} %pad_maximum_fusion.2), channel_id=1, source_target_pairs={{0,1},{1,2},{2,3},{3,4},{4,5},{5,6},{6,7},{7,8},{8,9},{9,10},{10,1... | collective-permute-start | bytes 4718600 | tf_op jit(solution)/shard_map/ppermute | solution.py:14
  289.8 33.6 %collective-permute-start.10 = (f32[3,1,1024,128]{2,3,1,0:T(8,128)}, f32[3,1,1024,128]{2,3,1,0:T(8,128)}, u32[]{:S(2)}, u32[]{:S(2)}) collective-permute-start(f32[3,1,1024,128]{2,3,1,0:T(8,128)} %pad_maximum_fusion.2), channel_id=1, source_target_pairs={{1,0},{2,1},{3,2},{4,3},{5,4},{6,5},{7,6},{8,7},{9,8},{10,9},{11,1... | collective-permute-start | bytes 4718600 | tf_op jit(solution)/shard_map/ppermute | solution.py:17
  339.7 29.7 %copy-start.7 = (f32[1024,128]{1,0:T(8,128)}, f32[1024,128]{1,0:T(8,128)S(1)}, u32[]{:S(2)}) copy-start(f32[1024,128]{1,0:T(8,128)S(1)} %scatter_custom_fusion.3) | copy-start | bytes 1572868
  341.5 383.9 %all-gather.17.cloned.1.call-start = ((), (), s32[]{:S(2)}) async-start(), calls=%async_computation.2 | async-start | bytes 8454144 | tf_op jit(solution)/shard_map/all_gather | solution.py:63
  466.2 179.7 %copy-start.3 = (f32[1,1,1024,128]{3,2,1,0:T(8,128)}, f32[1,1,1024,128]{3,2,1,0:T(8,128)S(1)}, u32[]{:S(2)}) copy-start(f32[1,1,1024,128]{3,2,1,0:T(8,128)S(1)} %fusion.16) | copy-start | bytes 1572868
  555.8 27.8 %collective-permute-start.12 = (f32[1,1,1024,128]{2,3,1,0:T(8,128)}, f32[1,1,1024,128]{2,3,1,0:T(8,128)S(1)}, u32[]{:S(2)}, u32[]{:S(2)}) collective-permute-start(f32[1,1,1024,128]{2,3,1,0:T(8,128)} %bitcast.413), channel_id=1, source_target_pairs={{0,16},{16,32},{32,48},{48,64},{64,80},{80,96},{96,112},{1,17},{17... | collective-permute-start | bytes 1572872 | tf_op jit(solution)/shard_map/ppermute | solution.py:14
  577.2 10.7 collective-permute-start.13
  583.6 6.8 copy-start.19
  587.9 2.5 copy-start.20
  590.4 31.3 %collective-permute-start.15 = (f32[3,1,1024,128]{2,3,1,0:T(8,128)}, f32[3,1,1024,128]{2,3,1,0:T(8,128)}, u32[]{:S(2)}, u32[]{:S(2)}) collective-permute-start(f32[3,1,1024,128]{2,3,1,0:T(8,128)} %pad_maximum_fusion.3), channel_id=1, source_target_pairs={{0,1},{1,2},{2,3},{3,4},{4,5},{5,6},{6,7},{7,8},{8,9},{9,10},{10,1... | collective-permute-start | bytes 4718600 | tf_op jit(solution)/shard_map/ppermute | solution.py:14
  594.6 34.0 %collective-permute-start.14 = (f32[3,1,1024,128]{2,3,1,0:T(8,128)}, f32[3,1,1024,128]{2,3,1,0:T(8,128)}, u32[]{:S(2)}, u32[]{:S(2)}) collective-permute-start(f32[3,1,1024,128]{2,3,1,0:T(8,128)} %pad_maximum_fusion.3), channel_id=1, source_target_pairs={{1,0},{2,1},{3,2},{4,3},{5,4},{6,5},{7,6},{8,7},{9,8},{10,9},{11,1... | collective-permute-start | bytes 4718600 | tf_op jit(solution)/shard_map/ppermute | solution.py:17
  648.7 232.8 %all-gather.19.cloned.1.call-start = ((), (), s32[]{:S(2)}) async-start(), calls=%async_computation.3 | async-start | bytes 8454144 | tf_op jit(solution)/shard_map/all_gather | solution.py:63
  733.8 13.9 %copy-start.10 = (f32[128,1024]{1,0:T(8,128)}, f32[128,1024]{1,0:T(8,128)S(1)}, u32[]{:S(2)}) copy-start(f32[128,1024]{1,0:T(8,128)S(1)} %fusion.2) | copy-start | bytes 1572868
  733.8 8.1 collective-permute-start.16
  735.8 10.5 collective-permute-start.17
  741.9 5.7 copy-start.21
  746.3 1.3 copy-start.22
  747.6 30.5 %collective-permute-start.19 = (f32[3,1,1024,128]{2,3,1,0:T(8,128)}, f32[3,1,1024,128]{2,3,1,0:T(8,128)}, u32[]{:S(2)}, u32[]{:S(2)}) collective-permute-start(f32[3,1,1024,128]{2,3,1,0:T(8,128)} %pad_maximum_fusion.4), channel_id=1, source_target_pairs={{0,1},{1,2},{2,3},{3,4},{4,5},{5,6},{6,7},{7,8},{8,9},{9,10},{10,1... | collective-permute-start | bytes 4718600 | tf_op jit(solution)/shard_map/ppermute | solution.py:14
  751.4 33.7 %collective-permute-start.18 = (f32[3,1,1024,128]{2,3,1,0:T(8,128)}, f32[3,1,1024,128]{2,3,1,0:T(8,128)}, u32[]{:S(2)}, u32[]{:S(2)}) collective-permute-start(f32[3,1,1024,128]{2,3,1,0:T(8,128)} %pad_maximum_fusion.4), channel_id=1, source_target_pairs={{1,0},{2,1},{3,2},{4,3},{5,4},{6,5},{7,6},{8,7},{9,8},{10,9},{11,1... | collective-permute-start | bytes 4718600 | tf_op jit(solution)/shard_map/ppermute | solution.py:17
  805.1 370.6 %all-gather.21.cloned.1.call-start = ((), (), s32[]{:S(2)}) async-start(), calls=%async_computation.4 | async-start | bytes 8454144 | tf_op jit(solution)/shard_map/all_gather | solution.py:63
  912.7 0.6 copy-start.29
  916.5 1.9 copy-start.1
  1006.7 27.2 %collective-permute-start.20 = (f32[1,1,1024,128]{2,3,1,0:T(8,128)}, f32[1,1,1024,128]{2,3,1,0:T(8,128)S(1)}, u32[]{:S(2)}, u32[]{:S(2)}) collective-permute-start(f32[1,1,1024,128]{2,3,1,0:T(8,128)} %bitcast.417), channel_id=1, source_target_pairs={{0,16},{16,32},{32,48},{48,64},{64,80},{80,96},{96,112},{1,17},{17... | collective-permute-start | bytes 1572872 | tf_op jit(solution)/shard_map/ppermute | solution.py:14
  1027.5 10.7 collective-permute-start.21
  1033.9 6.8 copy-start.23
  1038.2 2.5 copy-start.24
  1040.7 31.3 %collective-permute-start.23 = (f32[3,1,1024,128]{2,3,1,0:T(8,128)}, f32[3,1,1024,128]{2,3,1,0:T(8,128)}, u32[]{:S(2)}, u32[]{:S(2)}) collective-permute-start(f32[3,1,1024,128]{2,3,1,0:T(8,128)} %pad_maximum_fusion.5), channel_id=1, source_target_pairs={{0,1},{1,2},{2,3},{3,4},{4,5},{5,6},{6,7},{7,8},{8,9},{9,10},{10,1... | collective-permute-start | bytes 4718600 | tf_op jit(solution)/shard_map/ppermute | solution.py:14
  1044.9 34.0 %collective-permute-start.22 = (f32[3,1,1024,128]{2,3,1,0:T(8,128)}, f32[3,1,1024,128]{2,3,1,0:T(8,128)}, u32[]{:S(2)}, u32[]{:S(2)}) collective-permute-start(f32[3,1,1024,128]{2,3,1,0:T(8,128)} %pad_maximum_fusion.5), channel_id=1, source_target_pairs={{1,0},{2,1},{3,2},{4,3},{5,4},{6,5},{7,6},{8,7},{9,8},{10,9},{11,1... | collective-permute-start | bytes 4718600 | tf_op jit(solution)/shard_map/ppermute | solution.py:17
  1099.2 233.4 %all-gather.23.cloned.1.call-start = ((), (), s32[]{:S(2)}) async-start(), calls=%async_computation.5 | async-start | bytes 8454144 | tf_op jit(solution)/shard_map/all_gather | solution.py:63
  1181.7 2.6 copy-start.5
  1184.3 13.9 %copy-start.11 = (f32[128,1024]{1,0:T(8,128)}, f32[128,1024]{1,0:T(8,128)S(1)}, u32[]{:S(2)}) copy-start(f32[128,1024]{1,0:T(8,128)S(1)} %fusion) | copy-start | bytes 1572868
  1184.4 8.2 collective-permute-start.24
  1186.4 10.5 collective-permute-start.25
  1192.5 5.7 copy-start.25
  1196.9 1.3 copy-start.14
  1198.2 30.5 %collective-permute-start.27 = (f32[3,1,1024,128]{2,3,1,0:T(8,128)}, f32[3,1,1024,128]{2,3,1,0:T(8,128)}, u32[]{:S(2)}, u32[]{:S(2)}) collective-permute-start(f32[3,1,1024,128]{2,3,1,0:T(8,128)} %pad_maximum_fusion.6), channel_id=1, source_target_pairs={{0,1},{1,2},{2,3},{3,4},{4,5},{5,6},{6,7},{7,8},{8,9},{9,10},{10,1... | collective-permute-start | bytes 4718600 | tf_op jit(solution)/shard_map/ppermute | solution.py:14
  1202.0 33.7 %collective-permute-start.26 = (f32[3,1,1024,128]{2,3,1,0:T(8,128)}, f32[3,1,1024,128]{2,3,1,0:T(8,128)}, u32[]{:S(2)}, u32[]{:S(2)}) collective-permute-start(f32[3,1,1024,128]{2,3,1,0:T(8,128)} %pad_maximum_fusion.6), channel_id=1, source_target_pairs={{1,0},{2,1},{3,2},{4,3},{5,4},{6,5},{7,6},{8,7},{9,8},{10,9},{11,1... | collective-permute-start | bytes 4718600 | tf_op jit(solution)/shard_map/ppermute | solution.py:17
  1243.6 12.6 copy-start.28
  1332.6 27.5 %copy-start.2 = (f32[1,1,1024,128]{3,2,1,0:T(8,128)S(1)}, f32[1,1,1024,128]{3,2,1,0:T(8,128)}, u32[]{:S(2)}) copy-start(f32[1,1,1024,128]{3,2,1,0:T(8,128)} %copy-done.1) | copy-start | bytes 1572868
  1336.5 26.0 %copy-start.6 = (f32[1,1,1024,128]{3,2,1,0:T(8,128)S(1)}, f32[1,1,1024,128]{3,2,1,0:T(8,128)}, u32[]{:S(2)}) copy-start(f32[1,1,1024,128]{3,2,1,0:T(8,128)} %copy-done.5) | copy-start | bytes 1572868
  1359.6 2.9 copy-start.13
  (1 other events, 0.6 us)
Sparse Core Ops, SparseCore 0:
  261.4 104.1 all-gather.14
  369.3 67.1 all-gather.12
  648.8 76.5 all-gather.16
  805.3 76.2 all-gather.18
  1099.3 76.4 all-gather.20
  1256.3 76.2 all-gather.22
